TPU v7x, 512 devices: a whole 4x8x8 slice. The times are simulated.
512 devices in a mesh: src: 4 (over x_hi, core), depth: 8 (over y), lat: 16 (over z, x_lo).
Axes of the slice: x: 4 (x_hi: 2, x_lo: 2; x = x_hi * 2 + x_lo), y: 8, z: 8, core: 2. Of those that a mesh axis runs over, the one named last changes fastest.
Arguments:
- conductivity: float32 [128, 128, 128], P('depth', 'lat'), may hold values from 0.2 to 2
- e_start: float32 [8, 3, 128, 128, 128], P('src', None, 'depth', 'lat'), may hold values from -6 to 6
- h_start: float32 [8, 3, 128, 128, 128], P('src', None, 'depth', 'lat'), may hold values from -6 to 6
- e_weight: float32 [8, 3, 128, 128, 128], P('src', None, 'depth', 'lat'), may hold values from -6 to 6
- h_weight: float32 [8, 3, 128, 128, 128], P('src', None, 'depth', 'lat'), may hold values from -6 to 6
- source_amp: float32 [8, 3], P('src'), may hold values from -12 to 12
- tow_cell: int32 [8], P('src'), may hold values from 0 to 2097151
- rec_cell: int32 [8, 16, 16], P('depth', 'lat'), may hold values from 0 to 16383
- rec_owner: int32 [8, 16, 16, 1], P('depth', 'lat'), may hold values from 0 to 15; in each aligned block of 16 rows (0 to 15, 16 to 31, ..., all dimensions but the last counted through in order) at most 2 rows name the same one
Outputs:
- grad: float32 [128, 128, 128], P('depth', 'lat')
- line_samples: float32 [8, 8, 16, 16, 2, 9], P('src', 'depth', 'lat')
Inputs may be any that keep to these rules, and one draw needn't show every extreme that they name: `tow_cell`: a flat cell of the whole grid. `rec_cell`: a local flat cell of the receiver's block; cells may repeat. `rec_owner`: among the 16 receivers of one block, at most 2 have the same owner, and in some block exactly 2 do.
All inputs are finite; a program needn't handle non-finite values.
Results may differ from a plain program's by a relative error of at most 0.0003.
Values sent between devices are 32-bit elements; how exact they have to be, the bound alone decides.
No kernel may reach another device: no remote copies, remote signals or barrier semaphores. Data moves between devices by JAX's collectives and lax.ppermute only.
A program may use at most 128 MiB of HBM per device.

v0:
```python
import jax
import jax.numpy as jnp
from jax import lax
from jax.sharding import PartitionSpec as P

ch_coef = 0.5
loss_rate = 0.5


def passed_along(block, axis, distance):
    devices = range(lax.axis_size(axis))
    route = [(i - distance, i) for i in devices if i - distance in devices]
    return lax.ppermute(block, axis, route)


def component(field, k):
    return field[..., k, :, :, :]


def curl_upper(field, rim_z, rim_x):
    fx = component(field, 0)
    fy = component(field, 1)
    fz = component(field, 2)
    zx = jnp.concatenate([fx, component(rim_z, 0)], axis=-3)[..., 1:, :, :] - fx
    zy = jnp.concatenate([fy, component(rim_z, 1)], axis=-3)[..., 1:, :, :] - fy
    xy = jnp.concatenate([fy, component(rim_x, 0)], axis=-2)[..., :, 1:, :] - fy
    xz = jnp.concatenate([fz, component(rim_x, 1)], axis=-2)[..., :, 1:, :] - fz
    yz = jnp.concatenate([fz[..., 1:], jnp.zeros_like(fz[..., :1])], axis=-1) - fz
    yx = jnp.concatenate([fx[..., 1:], jnp.zeros_like(fx[..., :1])], axis=-1) - fx
    return jnp.stack([yz - zy, zx - xz, xy - yx], axis=-4)


def curl_lower(field, rim_z, rim_x):
    fx = component(field, 0)
    fy = component(field, 1)
    fz = component(field, 2)
    zx = fx - jnp.concatenate([component(rim_z, 0), fx], axis=-3)[..., :-1, :, :]
    zy = fy - jnp.concatenate([component(rim_z, 1), fy], axis=-3)[..., :-1, :, :]
    xy = fy - jnp.concatenate([component(rim_x, 0), fy], axis=-2)[..., :, :-1, :]
    xz = fz - jnp.concatenate([component(rim_x, 1), fz], axis=-2)[..., :, :-1, :]
    yz = fz - jnp.concatenate([jnp.zeros_like(fz[..., :1]), fz[..., :-1]], axis=-1)
    yx = fx - jnp.concatenate([jnp.zeros_like(fx[..., :1]), fx[..., :-1]], axis=-1)
    return jnp.stack([yz - zy, zx - xz, xy - yx], axis=-4)


def coefficients(sigma):
    denom = 1.0 + loss_rate * sigma
    decay = (1.0 - loss_rate * sigma) / denom
    gain = ch_coef / denom
    decay_slope = -2.0 * loss_rate / (denom * denom)
    gain_slope = -ch_coef * loss_rate / (denom * denom)
    return (decay, gain, decay_slope, gain_slope)


def upper_rims(field):
    rim_z = passed_along(field[:, 0:2, 0:1], "depth", -1)
    rim_x = passed_along(field[:, 1:3, :, 0:1], "lat", -1)
    return (rim_z, rim_x)


def lower_rims(field):
    rim_z = passed_along(field[:, 0:2, -1:], "depth", 1)
    rim_x = passed_along(field[:, 1:3, :, -1:], "lat", 1)
    return (rim_z, rim_x)


def leap_one(first, second, scale):
    scaled = scale * first
    rim_z, rim_x = upper_rims(scaled)
    updated = second + curl_upper(scaled, rim_z, rim_x)
    low_z, low_x = lower_rims(updated)
    return (updated, curl_lower(updated, low_z, low_x))


def per_device(
    conductivity, e_start, h_start, e_weight, h_weight, source_amp, tow_cell, rec_cell, rec_owner
):
    groups, _, depth_cells, lat_cells, width = e_start.shape
    steps_total = source_amp.shape[1]
    tiles = lax.axis_size("lat")
    capacity = max(2, rec_cell.shape[-1] // tiles)
    depth_at = lax.axis_index("depth")
    lat_at = lax.axis_index("lat")
    decay, gain, decay_slope, gain_slope = coefficients(conductivity)
    margin = 0
    decay_use, gain_use = (decay, gain)
    e_field, h_field, lam_e, lam_h = (e_start, h_start, e_weight, h_weight)

    def leap(first, second, scale):
        return leap_one(first, second, scale)

    plane = lat_cells * tiles * width
    local_z = tow_cell // plane - depth_at * depth_cells + margin
    local_x = tow_cell // width % (lat_cells * tiles) - lat_at * lat_cells + margin
    local_y = tow_cell % width
    grid_z = jnp.arange(depth_cells + 2 * margin)[:, None, None]
    grid_x = jnp.arange(lat_cells + 2 * margin)[None, :, None]
    grid_y = jnp.arange(width)[None, None, :]
    point = (
        (grid_z[None] == local_z[:, None, None, None])
        & (grid_x[None] == local_x[:, None, None, None])
        & (grid_y[None] == local_y[:, None, None, None])
    ).astype(jnp.float32)
    blank = jnp.zeros_like(point)
    owner = rec_owner.reshape(-1)
    cells = rec_cell.reshape(-1)
    order = jnp.arange(owner.shape[0])
    rank = jnp.sum(
        ((owner[:, None] == owner[None, :]) & (order[None, :] < order[:, None])).astype(jnp.int32),
        axis=1,
    )
    hot = (
        (owner[:, None, None] == jnp.arange(tiles)[:, None])
        & (rank[:, None, None] == jnp.arange(capacity)[None, :])
    ).astype(jnp.float32)
    kept = []
    delivered = []
    for step in range(steps_total):
        h_field, turned = leap(e_field, h_field, -ch_coef)
        source = source_amp[:, step][:, None, None, None] * point
        drive = turned - jnp.stack([source, blank, blank], axis=1)
        kept.append((e_field, drive))
        e_field = decay_use * e_field + gain_use * drive
        sampled = jnp.take(e_field.reshape(groups, 3, -1), cells, axis=2)
        placed = jnp.sum(sampled[:, :, :, None, None] * hot[None, None], axis=2)
        delivered.append(
            lax.all_to_all(
                jnp.transpose(placed, (0, 2, 3, 1)), "lat", split_axis=1, concat_axis=1, tiled=True
            )
        )
    received = jnp.concatenate(delivered, axis=-1)
    line_samples = received.reshape(groups, 1, 1, tiles, capacity, 3 * steps_total)
    local = jnp.zeros((depth_cells, lat_cells, width), jnp.float32)
    for step in range(steps_total - 1, -1, -1):
        e_old, drive = kept[step]
        weight_now = lam_e
        term = jnp.sum(
            decay_slope * e_old * weight_now + gain_slope * drive * weight_now, axis=(0, 1)
        )
        local = local + term
        if step > 0:
            lam_h, turned = leap(lam_e, lam_h, gain)
            lam_e = decay_use * lam_e - ch_coef * turned
    total = lax.psum(local, "src")
    return (total, line_samples)


def solution(mesh):
    placed = (
        P("depth", "lat", None),
        P("src", None, "depth", "lat", None),
        P("src", None, "depth", "lat", None),
        P("src", None, "depth", "lat", None),
        P("src", None, "depth", "lat", None),
        P("src", None),
        P("src"),
        P("depth", "lat", None),
        P("depth", "lat", None, None),
    )
    return jax.shard_map(
        per_device,
        mesh=mesh,
        in_specs=placed,
        out_specs=(P("depth", "lat", None), P("src", "depth", "lat", None, None, None)),
        check_vma=False,
    )
```

profile of v0, /device:TPU:1, one launch (start us, length us, event | category | flops | bytes accessed | tf_op | source)
XLA Modules:
  0.0 280.9 jit_solution(6807090759365684788)
XLA Ops:
  8.3 1.3 collective-permute-start
  9.6 1.3 collective-permute-start.1
  13.2 1.2 compare_and_fusion
  16.4 1.5 multiply_divide_fusion.1
  19.2 1.1 maximum_add_fusion
  20.3 4.7 %collective-permute-start.2 = (f32[2,2,1,8,128]{4,0,3,2,1:T(2,128)S(1)}, f32[2,2,1,8,128]{4,0,3,2,1:T(2,128)S(1)}, u32[]{:S(2)}, u32[]{:S(2)}) collective-permute-start(f32[2,2,1,8,128]{4,0,3,2,1:T(2,128)S(1)} %bitcast.362), channel_id=1, source_target_pairs={{0,16},{16,32},{32,48},{48,64},{64,80},{80,96},{96,112},{1,17},{17... | collective-permute-start | bytes 49160 | tf_op jit(solution)/shard_map/ppermute | solution.py:13
  25.0 4.0 %collective-permute-start.3 = (f32[2,2,16,1,128]{4,2,0,3,1:T(8,128)S(1)}, f32[2,2,16,1,128]{4,2,0,3,1:T(8,128)S(1)}, u32[]{:S(2)}, u32[]{:S(2)}) collective-permute-start(f32[2,2,16,1,128]{4,2,0,3,1:T(8,128)S(1)} %slice.636), channel_id=1, source_target_pairs={{0,1},{1,2},{2,3},{3,4},{4,5},{5,6},{6,7},{7,8},{8,9},{9,10},{10,1... | collective-permute-start | bytes 98312 | tf_op jit(solution)/shard_map/ppermute | solution.py:13
  30.3 1.2 multiply_add_fusion.2
  31.6 1.3 collective-permute-start.4
  33.0 11.4 %copy.327 = f32[2,3,16,8,128]{1,0,4,3,2:T(2,128)} copy(f32[2,3,16,8,128]{4,3,2,0,1:T(8,128)S(1)} %multiply_add_fusion.2) | data formatting | bytes 786432 | tf_op jit(solution)/shard_map/add | solution.py:123
  44.5 1.3 collective-permute-start.5
  46.0 6.9 %gather_fusion = f32[16,2,3]{2,1,0:T(2,128)} fusion(f32[2,3,16384]{1,0,2:T(2,128)} %bitcast.334, s32[1024]{0:T(1024)S(1)} %pad_clamp_fusion), kind=kCustom, calls=%fused_computation.clone | custom fusion | bytes 832 | tf_op jit(solution)/shard_map/jit(_take)/gather | solution.py:124
  53.7 4.0 %collective-permute-start.6 = (f32[2,2,1,8,128]{4,3,0,2,1:T(8,128)S(1)}, f32[2,2,1,8,128]{4,3,0,2,1:T(8,128)S(1)}, u32[]{:S(2)}, u32[]{:S(2)}) collective-permute-start(f32[2,2,1,8,128]{4,3,0,2,1:T(8,128)S(1)} %slice_bitcast_fusion.44), channel_id=1, source_target_pairs={{0,16},{16,32},{32,48},{48,64},{64,80},{80,96},{96,112},{1,17},{17... | collective-permute-start | bytes 49160 | tf_op jit(solution)/shard_map/ppermute | solution.py:13
  57.7 4.8 %collective-permute-start.7 = (f32[2,2,16,1,128]{4,3,2,0,1:T(1,128)S(1)}, f32[2,2,16,1,128]{4,3,2,0,1:T(1,128)S(1)}, u32[]{:S(2)}, u32[]{:S(2)}) collective-permute-start(f32[2,2,16,1,128]{4,3,2,0,1:T(1,128)S(1)} %slice.658), channel_id=1, source_target_pairs={{0,1},{1,2},{2,3},{3,4},{4,5},{5,6},{6,7},{7,8},{8,9},{9,10},{10,1... | collective-permute-start | bytes 98312 | tf_op jit(solution)/shard_map/ppermute | solution.py:13
  65.3 1.3 collective-permute-start.8
  70.6 1.3 collective-permute-start.9
  71.9 1.3 collective-permute-start.12
  74.7 1.3 collective-permute-start.13
  76.0 11.4 %copy.330 = f32[2,3,16,8,128]{1,0,4,3,2:T(2,128)} copy(f32[2,3,16,8,128]{4,3,2,0,1:T(8,128)S(1)} %get-tuple-element.18) | data formatting | bytes 786432 | tf_op jit(solution)/shard_map/add | solution.py:123
  87.4 7.1 %gather_fusion.1 = f32[16,2,3]{2,1,0:T(2,128)} fusion(f32[2,3,16384]{1,0,2:T(2,128)} %bitcast.336, s32[1024]{0:T(1024)} %copy-done.18), kind=kCustom, calls=%fused_computation.1.clone | custom fusion | bytes 832 | tf_op jit(solution)/shard_map/jit(_take)/gather | solution.py:124
  96.7 1.1 fusion.59
  97.8 1.2 fusion.63
  99.1 1.2 maximum_add_fusion.2
  100.4 4.6 %collective-permute-start.10 = (f32[2,2,1,8,128]{4,3,0,2,1:T(8,128)S(1)}, f32[2,2,1,8,128]{4,3,0,2,1:T(8,128)S(1)}, u32[]{:S(2)}, u32[]{:S(2)}) collective-permute-start(f32[2,2,1,8,128]{4,3,0,2,1:T(8,128)S(1)} %slice_bitcast_fusion.38), channel_id=1, source_target_pairs={{0,16},{16,32},{32,48},{48,64},{64,80},{80,96},{96,112},{1,17},{17... | collective-permute-start | bytes 49160 | tf_op jit(solution)/shard_map/ppermute | solution.py:13
  105.7 1.1 fusion.39
  106.9 1.3 fusion.43
  109.3 5.8 %collective-permute-start.11 = (f32[2,2,16,1,128]{4,3,2,0,1:T(1,128)S(1)}, f32[2,2,16,1,128]{4,3,2,0,1:T(1,128)S(1)}, u32[]{:S(2)}, u32[]{:S(2)}) collective-permute-start(f32[2,2,16,1,128]{4,3,2,0,1:T(1,128)S(1)} %slice.680), channel_id=1, source_target_pairs={{0,1},{1,2},{2,3},{3,4},{4,5},{5,6},{6,7},{7,8},{8,9},{9,10},{10,1... | collective-permute-start | bytes 98312 | tf_op jit(solution)/shard_map/ppermute | solution.py:13
  115.2 4.1 %collective-permute-start.14 = (f32[2,2,1,8,128]{4,3,0,2,1:T(8,128)S(1)}, f32[2,2,1,8,128]{4,3,0,2,1:T(8,128)S(1)}, u32[]{:S(2)}, u32[]{:S(2)}) collective-permute-start(f32[2,2,1,8,128]{4,3,0,2,1:T(8,128)S(1)} %copy.349), channel_id=1, source_target_pairs={{0,16},{16,32},{32,48},{48,64},{64,80},{80,96},{96,112},{1,17},{17... | collective-permute-start | bytes 49160 | tf_op jit(solution)/shard_map/ppermute | solution.py:13
  119.3 4.5 %collective-permute-start.15 = (f32[2,2,16,1,128]{4,2,0,3,1:T(8,128)S(1)}, f32[2,2,16,1,128]{4,2,0,3,1:T(8,128)S(1)}, u32[]{:S(2)}, u32[]{:S(2)}) collective-permute-start(f32[2,2,16,1,128]{4,2,0,3,1:T(8,128)S(1)} %copy.351), channel_id=1, source_target_pairs={{0,1},{1,2},{2,3},{3,4},{4,5},{5,6},{6,7},{7,8},{8,9},{9,10},{10,1... | collective-permute-start | bytes 98312 | tf_op jit(solution)/shard_map/ppermute | solution.py:13
  125.2 2.5 multiply_add_fusion
  127.7 12.7 %copy.333 = f32[2,3,16,8,128]{1,0,4,3,2:T(2,128)} copy(f32[2,3,16,8,128]{4,3,2,0,1:T(8,128)} %get-tuple-element.21) | data formatting | bytes 786432 | tf_op jit(solution)/shard_map/add | solution.py:123
  140.4 6.5 %gather_fusion.2 = f32[16,2,3]{2,1,0:T(2,128)S(1)} fusion(f32[2,3,16384]{1,0,2:T(2,128)} %bitcast.335, s32[1024]{0:T(1024)} %copy-done.18), kind=kCustom, calls=%fused_computation.2.clone | custom fusion | bytes 832 | tf_op jit(solution)/shard_map/jit(_take)/gather | solution.py:124
  148.2 14.6 %all-to-all-start.2 = ((f32[2,16,2,3]{3,2,0,1:T(2,128)}), f32[2,16,2,3]{3,2,0,1:T(2,128)S(1)}, u32[]{:S(2)}, u32[]{:S(2)}) async-start(f32[2,16,2,3]{3,2,0,1:T(2,128)} %copy.335), calls=%async_computation.2 | async-start | bytes 65536 | tf_op jit(solution)/shard_map/all_to_all | solution.py:127
  163.4 6.9 %all-to-all-done.2 = f32[2,16,2,3]{3,2,0,1:T(2,128)S(1)} async-done(((f32[2,16,2,3]{3,2,0,1:T(2,128)}), f32[2,16,2,3]{3,2,0,1:T(2,128)S(1)}, u32[]{:S(2)}, u32[]{:S(2)}) %all-to-all-start.2) | async-done | bytes 800 | tf_op jit(solution)/shard_map/all_to_all | solution.py:127
  170.3 3.5 %all-to-all-start.1 = ((f32[2,16,2,3]{3,2,0,1:T(2,128)}), f32[2,16,2,3]{3,2,0,1:T(2,128)S(1)}, u32[]{:S(2)}, u32[]{:S(2)}) async-start(f32[2,16,2,3]{3,2,0,1:T(2,128)} %copy.332), calls=%async_computation.1 | async-start | bytes 65536 | tf_op jit(solution)/shard_map/all_to_all | solution.py:127
  174.4 1.3 collective-permute-start.16
  176.4 5.0 %all-to-all-done.1 = f32[2,16,2,3]{3,2,0,1:T(2,128)S(1)} async-done(((f32[2,16,2,3]{3,2,0,1:T(2,128)}), f32[2,16,2,3]{3,2,0,1:T(2,128)S(1)}, u32[]{:S(2)}, u32[]{:S(2)}) %all-to-all-start.1) | async-done | bytes 800 | tf_op jit(solution)/shard_map/all_to_all | solution.py:127
  181.4 4.1 %all-to-all-start = ((f32[2,16,2,3]{3,2,0,1:T(2,128)}), f32[2,16,2,3]{3,2,0,1:T(2,128)}, u32[]{:S(2)}, u32[]{:S(2)}) async-start(f32[2,16,2,3]{3,2,0,1:T(2,128)} %copy.329), calls=%async_computation | async-start | bytes 65536 | tf_op jit(solution)/shard_map/all_to_all | solution.py:127
  187.1 1.3 collective-permute-start.17
  190.1 3.0 %all-to-all-done = f32[2,16,2,3]{3,2,0,1:T(2,128)} async-done(((f32[2,16,2,3]{3,2,0,1:T(2,128)}), f32[2,16,2,3]{3,2,0,1:T(2,128)}, u32[]{:S(2)}, u32[]{:S(2)}) %all-to-all-start) | async-done | bytes 800 | tf_op jit(solution)/shard_map/all_to_all | solution.py:127
  193.1 1.4 copy.336
  196.1 1.1 fusion.23
  197.3 4.6 %collective-permute-start.18 = (f32[2,2,1,8,128]{4,3,0,2,1:T(8,128)S(1)}, f32[2,2,1,8,128]{4,3,0,2,1:T(8,128)S(1)}, u32[]{:S(2)}, u32[]{:S(2)}) collective-permute-start(f32[2,2,1,8,128]{4,3,0,2,1:T(8,128)S(1)} %copy.355), channel_id=1, source_target_pairs={{0,16},{16,32},{32,48},{48,64},{64,80},{80,96},{96,112},{1,17},{17... | collective-permute-start | bytes 49160 | tf_op jit(solution)/shard_map/ppermute | solution.py:13
  202.0 2.2 collective-permute-start.19
  205.4 1.4 multiply_reduce_fusion
  207.5 1.3 maximum_bitcast_fusion
  208.8 63.8 %all-reduce.25.cloned.1.call-done = f32[16,8,128]{2,1,0:T(8,128)} async-done(((f32[16,8,128]{2,1,0:T(8,128)}), f32[16,8,128]{2,1,0:T(8,128)}) %all-reduce.25.cloned.1.call-update) | async-done | bytes 65552 | tf_op jit(solution)/shard_map/psum | solution.py:144
  272.6 1.5 copy.385
  (175 shorter events, 32.5 us)
Async XLA Ops:
  8.3 10.8 %collective-permute-start = (f32[2,2,1,8,128]{4,0,3,2,1:T(2,128)S(1)}, f32[2,2,1,8,128]{4,0,3,2,1:T(2,128)S(1)}, u32[]{:S(2)}, u32[]{:S(2)}) collective-permute-start(f32[2,2,1,8,128]{4,0,3,2,1:T(2,128)S(1)} %bitcast.361), channel_id=1, source_target_pairs={{16,0},{32,16},{48,32},{64,48},{80,64},{96,80},{112,96},{17,1},{33... | collective-permute-start | bytes 49160 | tf_op jit(solution)/shard_map/ppermute | solution.py:13
  9.6 9.5 %collective-permute-start.1 = (f32[2,2,16,1,128]{4,2,0,3,1:T(8,128)S(1)}, f32[2,2,16,1,128]{4,2,0,3,1:T(8,128)S(1)}, u32[]{:S(2)}, u32[]{:S(2)}) collective-permute-start(f32[2,2,16,1,128]{4,2,0,3,1:T(8,128)S(1)} %slice.625), channel_id=1, source_target_pairs={{1,0},{2,1},{3,2},{4,3},{5,4},{6,5},{7,6},{8,7},{9,8},{10,9},{11,1... | collective-permute-start | bytes 98312 | tf_op jit(solution)/shard_map/ppermute | solution.py:13
  18.8 11.5 %copy-start.12 = (f32[2,1,16,8,128]{4,3,2,0,1:T(8,128)}, f32[2,1,16,8,128]{4,3,2,0,1:T(8,128)S(1)}, u32[]{:S(2)}) copy-start(f32[2,1,16,8,128]{4,3,2,0,1:T(8,128)S(1)} %get-tuple-element.123) | copy-start | bytes 393220
  18.8 45.0 %copy-start.1 = (f32[2,3,16,8,128]{4,3,2,1,0:T(8,128)S(1)}, f32[2,3,16,8,128]{4,3,2,1,0:T(8,128)}, u32[]{:S(2)}) copy-start(f32[2,3,16,8,128]{4,3,2,1,0:T(8,128)} %param.14) | copy-start | bytes 1179652
  18.8 34.2 %copy-start.18 = (s32[1024]{0:T(1024)}, s32[1024]{0:T(1024)S(1)}, u32[]{:S(2)}) copy-start(s32[1024]{0:T(1024)S(1)} %pad_clamp_fusion) | copy-start | bytes 12292
  20.3 8.7 %collective-permute-start.2 = (f32[2,2,1,8,128]{4,0,3,2,1:T(2,128)S(1)}, f32[2,2,1,8,128]{4,0,3,2,1:T(2,128)S(1)}, u32[]{:S(2)}, u32[]{:S(2)}) collective-permute-start(f32[2,2,1,8,128]{4,0,3,2,1:T(2,128)S(1)} %bitcast.362), channel_id=1, source_target_pairs={{0,16},{16,32},{32,48},{48,64},{64,80},{80,96},{96,112},{1,17},{17... | collective-permute-start | bytes 49160 | tf_op jit(solution)/shard_map/ppermute | solution.py:13
  25.0 5.0 %collective-permute-start.3 = (f32[2,2,16,1,128]{4,2,0,3,1:T(8,128)S(1)}, f32[2,2,16,1,128]{4,2,0,3,1:T(8,128)S(1)}, u32[]{:S(2)}, u32[]{:S(2)}) collective-permute-start(f32[2,2,16,1,128]{4,2,0,3,1:T(8,128)S(1)} %slice.636), channel_id=1, source_target_pairs={{0,1},{1,2},{2,3},{3,4},{4,5},{5,6},{6,7},{7,8},{8,9},{9,10},{10,1... | collective-permute-start | bytes 98312 | tf_op jit(solution)/shard_map/ppermute | solution.py:13
  31.6 21.4 %collective-permute-start.4 = (f32[2,2,1,8,128]{4,2,0,3,1:T(1,128)S(1)}, f32[2,2,1,8,128]{4,2,0,3,1:T(1,128)S(1)}, u32[]{:S(2)}, u32[]{:S(2)}) collective-permute-start(f32[2,2,1,8,128]{4,2,0,3,1:T(1,128)S(1)} %slice.643), channel_id=1, source_target_pairs={{16,0},{32,16},{48,32},{64,48},{80,64},{96,80},{112,96},{17,1},{33... | collective-permute-start | bytes 49160 | tf_op jit(solution)/shard_map/ppermute | solution.py:13
  44.5 8.5 %collective-permute-start.5 = (f32[2,2,16,1,128]{4,2,0,3,1:T(8,128)S(1)}, f32[2,2,16,1,128]{4,2,0,3,1:T(8,128)S(1)}, u32[]{:S(2)}, u32[]{:S(2)}) collective-permute-start(f32[2,2,16,1,128]{4,2,0,3,1:T(8,128)S(1)} %slice.647), channel_id=1, source_target_pairs={{1,0},{2,1},{3,2},{4,3},{5,4},{6,5},{7,6},{8,7},{9,8},{10,9},{11,1... | collective-permute-start | bytes 98312 | tf_op jit(solution)/shard_map/ppermute | solution.py:13
  53.2 10.6 %copy-start.6 = (f32[2,1,16,8,128]{4,3,2,0,1:T(8,128)}, f32[2,1,16,8,128]{4,3,2,0,1:T(8,128)S(1)}, u32[]{:S(2)}) copy-start(f32[2,1,16,8,128]{4,3,2,0,1:T(8,128)S(1)} %copy.285) | copy-start | bytes 393220
  53.3 10.4 %copy-start.7 = (f32[2,1,16,8,128]{4,3,2,0,1:T(8,128)}, f32[2,1,16,8,128]{4,3,2,0,1:T(8,128)S(1)}, u32[]{:S(2)}) copy-start(f32[2,1,16,8,128]{4,3,2,0,1:T(8,128)S(1)} %fusion.102) | copy-start | bytes 393220
  53.7 8.9 %collective-permute-start.6 = (f32[2,2,1,8,128]{4,3,0,2,1:T(8,128)S(1)}, f32[2,2,1,8,128]{4,3,0,2,1:T(8,128)S(1)}, u32[]{:S(2)}, u32[]{:S(2)}) collective-permute-start(f32[2,2,1,8,128]{4,3,0,2,1:T(8,128)S(1)} %slice_bitcast_fusion.44), channel_id=1, source_target_pairs={{0,16},{16,32},{32,48},{48,64},{64,80},{80,96},{96,112},{1,17},{17... | collective-permute-start | bytes 49160 | tf_op jit(solution)/shard_map/ppermute | solution.py:13
  57.7 5.8 %collective-permute-start.7 = (f32[2,2,16,1,128]{4,3,2,0,1:T(1,128)S(1)}, f32[2,2,16,1,128]{4,3,2,0,1:T(1,128)S(1)}, u32[]{:S(2)}, u32[]{:S(2)}) collective-permute-start(f32[2,2,16,1,128]{4,3,2,0,1:T(1,128)S(1)} %slice.658), channel_id=1, source_target_pairs={{0,1},{1,2},{2,3},{3,4},{4,5},{5,6},{6,7},{7,8},{8,9},{9,10},{10,1... | collective-permute-start | bytes 98312 | tf_op jit(solution)/shard_map/ppermute | solution.py:13
  63.7 61.5 %copy-start.2 = (f32[2,1,16,8,128]{4,3,2,0,1:T(8,128)}, f32[2,1,16,8,128]{4,3,2,0,1:T(8,128)S(1)}, u32[]{:S(2)}) copy-start(f32[2,1,16,8,128]{4,3,2,0,1:T(8,128)S(1)} %get-tuple-element.33) | copy-start | bytes 393220
  63.7 61.5 %copy-start.4 = (f32[2,1,16,8,128]{4,3,2,0,1:T(8,128)}, f32[2,1,16,8,128]{4,3,2,0,1:T(8,128)S(1)}, u32[]{:S(2)}) copy-start(f32[2,1,16,8,128]{4,3,2,0,1:T(8,128)S(1)} %get-tuple-element.34) | copy-start | bytes 393220
  64.6 10.1 %copy-start.10 = (f32[2,16,8,128]{3,2,1,0:T(8,128)}, f32[2,16,8,128]{3,2,1,0:T(8,128)S(1)}, u32[]{:S(2)}) copy-start(f32[2,16,8,128]{3,2,1,0:T(8,128)S(1)} %get-tuple-element.46) | copy-start | bytes 393220
  64.6 11.4 %copy-start.11 = (f32[2,16,8,128]{3,2,1,0:T(8,128)}, f32[2,16,8,128]{3,2,1,0:T(8,128)S(1)}, u32[]{:S(2)}) copy-start(f32[2,16,8,128]{3,2,1,0:T(8,128)S(1)} %get-tuple-element.47) | copy-start | bytes 393220
  65.3 29.2 %collective-permute-start.8 = (f32[2,2,1,8,128]{4,3,0,2,1:T(8,128)}, f32[2,2,1,8,128]{4,3,0,2,1:T(8,128)}, u32[]{:S(2)}, u32[]{:S(2)}) collective-permute-start(f32[2,2,1,8,128]{4,3,0,2,1:T(8,128)} %slice_bitcast_fusion.41), channel_id=1, source_target_pairs={{16,0},{32,16},{48,32},{64,48},{80,64},{96,80},{112,96},{17,1},{33... | collective-permute-start | bytes 49160 | tf_op jit(solution)/shard_map/ppermute | solution.py:13
  67.2 6.0 %copy-start.8 = (f32[2,16,8,128]{3,2,1,0:T(8,128)}, f32[2,16,8,128]{3,2,1,0:T(8,128)S(1)}, u32[]{:S(2)}) copy-start(f32[2,16,8,128]{3,2,1,0:T(8,128)S(1)} %get-tuple-element.71) | copy-start | bytes 393220
  67.2 6.7 %copy-start.9 = (f32[2,16,8,128]{3,2,1,0:T(8,128)}, f32[2,16,8,128]{3,2,1,0:T(8,128)S(1)}, u32[]{:S(2)}) copy-start(f32[2,16,8,128]{3,2,1,0:T(8,128)S(1)} %get-tuple-element.72) | copy-start | bytes 393220
  70.6 25.3 %collective-permute-start.9 = (f32[2,2,16,1,128]{4,3,2,0,1:T(1,128)}, f32[2,2,16,1,128]{4,3,2,0,1:T(1,128)}, u32[]{:S(2)}, u32[]{:S(2)}) collective-permute-start(f32[2,2,16,1,128]{4,3,2,0,1:T(1,128)} %slice.669), channel_id=1, source_target_pairs={{1,0},{2,1},{3,2},{4,3},{5,4},{6,5},{7,6},{8,7},{9,8},{10,9},{11,1... | collective-permute-start | bytes 98312 | tf_op jit(solution)/shard_map/ppermute | solution.py:13
  71.9 23.3 %collective-permute-start.12 = (f32[2,2,1,8,128]{4,3,0,2,1:T(8,128)}, f32[2,2,1,8,128]{4,3,0,2,1:T(8,128)}, u32[]{:S(2)}, u32[]{:S(2)}) collective-permute-start(f32[2,2,1,8,128]{4,3,0,2,1:T(8,128)} %slice_bitcast_fusion.35), channel_id=1, source_target_pairs={{16,0},{32,16},{48,32},{64,48},{80,64},{96,80},{112,96},{17,1},{33... | collective-permute-start | bytes 49160 | tf_op jit(solution)/shard_map/ppermute | solution.py:13
  74.7 30.2 %collective-permute-start.13 = (f32[2,2,16,1,128]{4,3,2,0,1:T(1,128)}, f32[2,2,16,1,128]{4,3,2,0,1:T(1,128)}, u32[]{:S(2)}, u32[]{:S(2)}) collective-permute-start(f32[2,2,16,1,128]{4,3,2,0,1:T(1,128)} %slice.691), channel_id=1, source_target_pairs={{1,0},{2,1},{3,2},{4,3},{5,4},{6,5},{7,6},{8,7},{9,8},{10,9},{11,1... | collective-permute-start | bytes 98312 | tf_op jit(solution)/shard_map/ppermute | solution.py:13
  100.4 23.5 %collective-permute-start.10 = (f32[2,2,1,8,128]{4,3,0,2,1:T(8,128)S(1)}, f32[2,2,1,8,128]{4,3,0,2,1:T(8,128)S(1)}, u32[]{:S(2)}, u32[]{:S(2)}) collective-permute-start(f32[2,2,1,8,128]{4,3,0,2,1:T(8,128)S(1)} %slice_bitcast_fusion.38), channel_id=1, source_target_pairs={{0,16},{16,32},{32,48},{48,64},{64,80},{80,96},{96,112},{1,17},{17... | collective-permute-start | bytes 49160 | tf_op jit(solution)/shard_map/ppermute | solution.py:13
  106.9 98.5 %copy-start = (f32[2,3,16,8,128]{4,3,2,1,0:T(8,128)S(1)}, f32[2,3,16,8,128]{4,3,2,1,0:T(8,128)}, u32[]{:S(2)}) copy-start(f32[2,3,16,8,128]{4,3,2,1,0:T(8,128)} %param.12) | copy-start | bytes 1179652
  109.3 14.6 %collective-permute-start.11 = (f32[2,2,16,1,128]{4,3,2,0,1:T(1,128)S(1)}, f32[2,2,16,1,128]{4,3,2,0,1:T(1,128)S(1)}, u32[]{:S(2)}, u32[]{:S(2)}) collective-permute-start(f32[2,2,16,1,128]{4,3,2,0,1:T(1,128)S(1)} %slice.680), channel_id=1, source_target_pairs={{0,1},{1,2},{2,3},{3,4},{4,5},{5,6},{6,7},{7,8},{8,9},{9,10},{10,1... | collective-permute-start | bytes 98312 | tf_op jit(solution)/shard_map/ppermute | solution.py:13
  115.2 8.7 %collective-permute-start.14 = (f32[2,2,1,8,128]{4,3,0,2,1:T(8,128)S(1)}, f32[2,2,1,8,128]{4,3,0,2,1:T(8,128)S(1)}, u32[]{:S(2)}, u32[]{:S(2)}) collective-permute-start(f32[2,2,1,8,128]{4,3,0,2,1:T(8,128)S(1)} %copy.349), channel_id=1, source_target_pairs={{0,16},{16,32},{32,48},{48,64},{64,80},{80,96},{96,112},{1,17},{17... | collective-permute-start | bytes 49160 | tf_op jit(solution)/shard_map/ppermute | solution.py:13
  119.3 5.6 %collective-permute-start.15 = (f32[2,2,16,1,128]{4,2,0,3,1:T(8,128)S(1)}, f32[2,2,16,1,128]{4,2,0,3,1:T(8,128)S(1)}, u32[]{:S(2)}, u32[]{:S(2)}) collective-permute-start(f32[2,2,16,1,128]{4,2,0,3,1:T(8,128)S(1)} %copy.351), channel_id=1, source_target_pairs={{0,1},{1,2},{2,3},{3,4},{4,5},{5,6},{6,7},{7,8},{8,9},{9,10},{10,1... | collective-permute-start | bytes 98312 | tf_op jit(solution)/shard_map/ppermute | solution.py:13
  127.7 19.2 %copy-start.16 = (f32[16,2,3]{2,1,0:T(2,128)S(1)}, f32[16,2,3]{2,1,0:T(2,128)}, u32[]{:S(2)}) copy-start(f32[16,2,3]{2,1,0:T(2,128)} %gather_fusion) | copy-start | bytes 1156
  127.7 19.2 %copy-start.17 = (f32[16,2,3]{2,1,0:T(2,128)S(1)}, f32[16,2,3]{2,1,0:T(2,128)}, u32[]{:S(2)}) copy-start(f32[16,2,3]{2,1,0:T(2,128)} %gather_fusion.1) | copy-start | bytes 1156
  127.7 19.2 %copy-start.19 = (pred[16]{0:T(512)(128)(4,1)S(1)}, pred[16]{0:T(512)(128)(4,1)}, u32[]{:S(2)}) copy-start(pred[16]{0:T(512)(128)(4,1)} %compare_and_fusion) | copy-start | bytes 52
  127.7 77.7 %copy-start.3 = (f32[2,1,16,8,128]{4,3,2,0,1:T(8,128)S(1)}, f32[2,1,16,8,128]{4,3,2,0,1:T(8,128)}, u32[]{:S(2)}) copy-start(f32[2,1,16,8,128]{4,3,2,0,1:T(8,128)} %copy-done.2) | copy-start | bytes 393220
  127.7 77.7 %copy-start.5 = (f32[2,1,16,8,128]{4,3,2,0,1:T(8,128)S(1)}, f32[2,1,16,8,128]{4,3,2,0,1:T(8,128)}, u32[]{:S(2)}) copy-start(f32[2,1,16,8,128]{4,3,2,0,1:T(8,128)} %copy-done.4) | copy-start | bytes 393220
  127.7 79.1 %copy-start.13 = (f32[16,8,128]{2,1,0:T(8,128)S(1)}, f32[16,8,128]{2,1,0:T(8,128)}, u32[]{:S(2)}) copy-start(f32[16,8,128]{2,1,0:T(8,128)} %get-tuple-element.22) | copy-start | bytes 196612
  148.2 22.2 %all-to-all-start.2 = ((f32[2,16,2,3]{3,2,0,1:T(2,128)}), f32[2,16,2,3]{3,2,0,1:T(2,128)S(1)}, u32[]{:S(2)}, u32[]{:S(2)}) async-start(f32[2,16,2,3]{3,2,0,1:T(2,128)} %copy.335), calls=%async_computation.2 | async-start | bytes 65536 | tf_op jit(solution)/shard_map/all_to_all | solution.py:127
  170.3 15.2 %copy-start.14 = (f32[2,16,2,3]{3,2,0,1:T(2,128)}, f32[2,16,2,3]{3,2,0,1:T(2,128)S(1)}, u32[]{:S(2)}) copy-start(f32[2,16,2,3]{3,2,0,1:T(2,128)S(1)} %all-to-all-done.2) | copy-start | bytes 2308
  170.3 11.1 %all-to-all-start.1 = ((f32[2,16,2,3]{3,2,0,1:T(2,128)}), f32[2,16,2,3]{3,2,0,1:T(2,128)S(1)}, u32[]{:S(2)}, u32[]{:S(2)}) async-start(f32[2,16,2,3]{3,2,0,1:T(2,128)} %copy.332), calls=%async_computation.1 | async-start | bytes 65536 | tf_op jit(solution)/shard_map/all_to_all | solution.py:127
  174.4 20.1 %collective-permute-start.16 = (f32[2,2,1,8,128]{4,3,0,2,1:T(8,128)}, f32[2,2,1,8,128]{4,3,0,2,1:T(8,128)}, u32[]{:S(2)}, u32[]{:S(2)}) collective-permute-start(f32[2,2,1,8,128]{4,3,0,2,1:T(8,128)} %slice_bitcast_fusion.32), channel_id=1, source_target_pairs={{16,0},{32,16},{48,32},{64,48},{80,64},{96,80},{112,96},{17,1},{33... | collective-permute-start | bytes 49160 | tf_op jit(solution)/shard_map/ppermute | solution.py:13
  181.4 4.1 %copy-start.15 = (f32[2,16,2,3]{3,2,0,1:T(2,128)}, f32[2,16,2,3]{3,2,0,1:T(2,128)S(1)}, u32[]{:S(2)}) copy-start(f32[2,16,2,3]{3,2,0,1:T(2,128)S(1)} %all-to-all-done.1) | copy-start | bytes 2308
  181.4 11.7 %all-to-all-start = ((f32[2,16,2,3]{3,2,0,1:T(2,128)}), f32[2,16,2,3]{3,2,0,1:T(2,128)}, u32[]{:S(2)}, u32[]{:S(2)}) async-start(f32[2,16,2,3]{3,2,0,1:T(2,128)} %copy.329), calls=%async_computation | async-start | bytes 65536 | tf_op jit(solution)/shard_map/all_to_all | solution.py:127
  185.6 87.0 %all-reduce.25.cloned.1.call-start = ((), (), s32[]{:S(2)}) async-start(), calls=%async_computation.3 | async-start | bytes 131072 | tf_op jit(solution)/shard_map/psum | solution.py:144
  187.1 8.2 %collective-permute-start.17 = (f32[2,2,16,1,128]{4,3,2,0,1:T(1,128)}, f32[2,2,16,1,128]{4,3,2,0,1:T(1,128)}, u32[]{:S(2)}, u32[]{:S(2)}) collective-permute-start(f32[2,2,16,1,128]{4,3,2,0,1:T(1,128)} %slice.713), channel_id=1, source_target_pairs={{1,0},{2,1},{3,2},{4,3},{5,4},{6,5},{7,6},{8,7},{9,8},{10,9},{11,1... | collective-permute-start | bytes 98312 | tf_op jit(solution)/shard_map/ppermute | solution.py:13
  197.3 6.9 %collective-permute-start.18 = (f32[2,2,1,8,128]{4,3,0,2,1:T(8,128)S(1)}, f32[2,2,1,8,128]{4,3,0,2,1:T(8,128)S(1)}, u32[]{:S(2)}, u32[]{:S(2)}) collective-permute-start(f32[2,2,1,8,128]{4,3,0,2,1:T(8,128)S(1)} %copy.355), channel_id=1, source_target_pairs={{0,16},{16,32},{32,48},{48,64},{64,80},{80,96},{96,112},{1,17},{17... | collective-permute-start | bytes 49160 | tf_op jit(solution)/shard_map/ppermute | solution.py:13
  202.0 3.2 %collective-permute-start.19 = (f32[2,2,16,1,128]{4,3,2,1,0:T(1,128)S(1)}, f32[2,2,16,1,128]{4,3,2,1,0:T(1,128)S(1)}, u32[]{:S(2)}, u32[]{:S(2)}) collective-permute-start(f32[2,2,16,1,128]{4,3,2,1,0:T(1,128)S(1)} %slice.724), channel_id=1, source_target_pairs={{0,1},{1,2},{2,3},{3,4},{4,5},{5,6},{6,7},{7,8},{8,9},{9,10},{10,1... | collective-permute-start | bytes 98312 | tf_op jit(solution)/shard_map/ppermute | solution.py:13
Sparse Core Ops, SparseCore 0:
  207.6 64.9 all-reduce.24
where the time goes:
time: 284 us; the launch traced here: 281 us
  waiting for transfers between devices  82.6 us (29%)
  local copies, waits for them, and re-layouts  78.5 us (28%)
  starting transfers between devices  78.4 us (28%)
  other arithmetic  26.5 us (9%)
  between operations  15 us (5%)
    psum x1, waiting for transfers between devices, per_device(): total = lax.psum(local, 'src')  63.8 us
    ppermute x20, starting transfers between devices, passed_along(): return lax.ppermute(block, axis, route)  56.2 us
    add x3, local copies, waits for them, and re-layouts, per_device(): e_field = decay_use * e_field + gain_use * drive  35.4 us
    all_to_all x3, starting transfers between devices, per_device(): lax.all_to_all(jnp.transpose(placed, (0, 2, 3, 1)), 'lat', split_axis=1,...  22.2 us
    gather x3, local copies, waits for them, and re-layouts, per_device(): sampled = jnp.take(e_field.reshape(groups, 3, -1), cells, axis=2)  20.5 us
    all_to_all x3, waiting for transfers between devices, per_device(): lax.all_to_all(jnp.transpose(placed, (0, 2, 3, 1)), 'lat', split_axis=1,...  14.9 us
    squeeze x27, local copies, waits for them, and re-layouts, component(): return field[..., k, :, :, :]  6.66 us
    another operation x10, other arithmetic, curl_upper(): return jnp.stack([yz - zy, zx - xz, xy - yx], axis=-4)  6.36 us
  transfers between devices with their start and end apart: 24, of which 8 were waited for; matrix products, arithmetic and copies ran while one was open for 25% of the time, Pallas kernels for 0%

commit v1 on v0

--- a/solution.py
+++ b/solution.py
@@ -2,6 +2,7 @@
 import jax.numpy as jnp
 from jax import lax
 from jax.sharding import PartitionSpec as P
+from jax.lax import all_gather
 
 ch_coef = 0.5
 loss_rate = 0.5
@@ -141,7 +142,12 @@
         if step > 0:
             lam_h, turned = leap(lam_e, lam_h, gain)
             lam_e = decay_use * lam_e - ch_coef * turned
-    total = lax.psum(local, "src")
+
+    def pack_the_regions(panel):
+        tmp = all_gather(panel, "src")
+        return jnp.sum(tmp, 0)
+
+    total = pack_the_regions(local)
     return (total, line_samples)
 
 

time: 284 us -> 229 us (0.81)
  the two profiles are of different devices: /device:TPU:1 before, /device:TPU:89 now
where the time goes in v1:
time: 229 us; the launch traced here: 226 us
  starting transfers between devices  81.2 us (35%)
  local copies, waits for them, and re-layouts  77.3 us (34%)
  other arithmetic  26.4 us (12%)
  waiting for transfers between devices  20.1 us (9%)
  blocking collectives  19.5 us (9%)
    ppermute x20, starting transfers between devices, passed_along(): return lax.ppermute(block, axis, route)  58.5 us
    add x3, local copies, waits for them, and re-layouts, per_device(): e_field = decay_use * e_field + gain_use * drive  35.7 us
    all_to_all x3, starting transfers between devices, per_device(): lax.all_to_all(jnp.transpose(placed, (0, 2, 3, 1)), 'lat', split_axis=1,...  22.7 us
    gather x3, local copies, waits for them, and re-layouts, per_device(): sampled = jnp.take(e_field.reshape(groups, 3, -1), cells, axis=2)  20.5 us
    all_gather x1, blocking collectives, pack_the_regions(): tmp = all_gather(panel, 'src')  19.5 us
    all_to_all x3, waiting for transfers between devices, per_device(): lax.all_to_all(jnp.transpose(placed, (0, 2, 3, 1)), 'lat', split_axis=1,...  10.9 us
    ppermute x20, waiting for transfers between devices, passed_along(): return lax.ppermute(block, axis, route)  9.17 us
    squeeze x27, local copies, waits for them, and re-layouts, component(): return field[..., k, :, :, :]  6.66 us
  transfers between devices with their start and end apart: 23, of which 6 were waited for; matrix products, arithmetic and copies ran while one was open for 31% of the time, Pallas kernels for 0%

profile of v1, /device:TPU:89, one launch (start us, length us, event | category | flops | bytes accessed | tf_op | source)
XLA Modules:
  0.0 226.1 jit_solution(9767252880703992162)
XLA Ops:
  1.7 2.1 collective-permute-start
  3.8 2.2 collective-permute-start.1
  8.4 1.2 compare_and_fusion
  11.5 1.5 multiply_divide_fusion.1
  15.4 4.4 %collective-permute-start.2 = (f32[2,2,1,8,128]{4,0,3,2,1:T(2,128)S(1)}, f32[2,2,1,8,128]{4,0,3,2,1:T(2,128)S(1)}, u32[]{:S(2)}, u32[]{:S(2)}) collective-permute-start(f32[2,2,1,8,128]{4,0,3,2,1:T(2,128)S(1)} %bitcast.364), channel_id=1, source_target_pairs={{0,16},{16,32},{32,48},{48,64},{64,80},{80,96},{96,112},{1,17},{17... | collective-permute-start | bytes 49160 | tf_op jit(solution)/shard_map/ppermute | solution.py:14
  19.9 3.1 %collective-permute-start.3 = (f32[2,2,16,1,128]{4,2,0,3,1:T(8,128)S(1)}, f32[2,2,16,1,128]{4,2,0,3,1:T(8,128)S(1)}, u32[]{:S(2)}, u32[]{:S(2)}) collective-permute-start(f32[2,2,16,1,128]{4,2,0,3,1:T(8,128)S(1)} %slice.636), channel_id=1, source_target_pairs={{0,1},{1,2},{2,3},{3,4},{4,5},{5,6},{6,7},{7,8},{8,9},{9,10},{10,1... | collective-permute-start | bytes 98312 | tf_op jit(solution)/shard_map/ppermute | solution.py:14
  23.0 2.5 %collective-permute-done.3 = f32[2,2,16,1,128]{4,2,0,3,1:T(8,128)S(1)} collective-permute-done((f32[2,2,16,1,128]{4,2,0,3,1:T(8,128)S(1)}, f32[2,2,16,1,128]{4,2,0,3,1:T(8,128)S(1)}, u32[]{:S(2)}, u32[]{:S(2)}) %collective-permute-start.3) | collective-permute-done | bytes 32800 | tf_op jit(solution)/shard_map/ppermute | solution.py:14
  25.7 1.2 multiply_add_fusion.2
  27.0 1.9 collective-permute-start.4
  29.0 11.5 %copy.327 = f32[2,3,16,8,128]{1,0,4,3,2:T(2,128)} copy(f32[2,3,16,8,128]{4,3,2,0,1:T(8,128)S(1)} %multiply_add_fusion.2) | data formatting | bytes 786432 | tf_op jit(solution)/shard_map/add | solution.py:124
  40.6 1.9 collective-permute-start.5
  42.8 6.9 %gather_fusion = f32[16,2,3]{2,1,0:T(2,128)} fusion(f32[2,3,16384]{1,0,2:T(2,128)} %bitcast.335, s32[1024]{0:T(1024)S(1)} %pad_clamp_fusion), kind=kCustom, calls=%fused_computation.clone | custom fusion | bytes 832 | tf_op jit(solution)/shard_map/jit(_take)/gather | solution.py:125
  50.4 4.6 %collective-permute-start.6 = (f32[2,2,1,8,128]{4,3,0,2,1:T(8,128)S(1)}, f32[2,2,1,8,128]{4,3,0,2,1:T(8,128)S(1)}, u32[]{:S(2)}, u32[]{:S(2)}) collective-permute-start(f32[2,2,1,8,128]{4,3,0,2,1:T(8,128)S(1)} %slice_bitcast_fusion.44), channel_id=1, source_target_pairs={{0,16},{16,32},{32,48},{48,64},{64,80},{80,96},{96,112},{1,17},{17... | collective-permute-start | bytes 49160 | tf_op jit(solution)/shard_map/ppermute | solution.py:14
  55.1 3.4 %collective-permute-start.7 = (f32[2,2,16,1,128]{4,3,2,0,1:T(1,128)S(1)}, f32[2,2,16,1,128]{4,3,2,0,1:T(1,128)S(1)}, u32[]{:S(2)}, u32[]{:S(2)}) collective-permute-start(f32[2,2,16,1,128]{4,3,2,0,1:T(1,128)S(1)} %slice.658), channel_id=1, source_target_pairs={{0,1},{1,2},{2,3},{3,4},{4,5},{5,6},{6,7},{7,8},{8,9},{9,10},{10,1... | collective-permute-start | bytes 98312 | tf_op jit(solution)/shard_map/ppermute | solution.py:14
  58.5 2.2 collective-permute-done.7
  62.3 1.9 collective-permute-start.8
  68.4 1.9 collective-permute-start.9
  70.3 1.9 collective-permute-start.12
  73.7 1.9 collective-permute-start.13
  75.7 11.5 %copy.330 = f32[2,3,16,8,128]{1,0,4,3,2:T(2,128)} copy(f32[2,3,16,8,128]{4,3,2,0,1:T(8,128)S(1)} %get-tuple-element.18) | data formatting | bytes 786432 | tf_op jit(solution)/shard_map/add | solution.py:124
  87.1 7.1 %gather_fusion.1 = f32[16,2,3]{2,1,0:T(2,128)} fusion(f32[2,3,16384]{1,0,2:T(2,128)} %bitcast.337, s32[1024]{0:T(1024)} %copy-done.18), kind=kCustom, calls=%fused_computation.1.clone | custom fusion | bytes 832 | tf_op jit(solution)/shard_map/jit(_take)/gather | solution.py:125
  96.4 1.1 fusion.59
  97.5 1.2 fusion.63
  98.8 1.2 maximum_add_fusion.2
  100.1 4.6 %collective-permute-start.10 = (f32[2,2,1,8,128]{4,3,0,2,1:T(8,128)S(1)}, f32[2,2,1,8,128]{4,3,0,2,1:T(8,128)S(1)}, u32[]{:S(2)}, u32[]{:S(2)}) collective-permute-start(f32[2,2,1,8,128]{4,3,0,2,1:T(8,128)S(1)} %slice_bitcast_fusion.38), channel_id=1, source_target_pairs={{0,16},{16,32},{32,48},{48,64},{64,80},{80,96},{96,112},{1,17},{17... | collective-permute-start | bytes 49160 | tf_op jit(solution)/shard_map/ppermute | solution.py:14
  105.4 1.1 fusion.39
  106.5 1.3 fusion.43
  109.0 3.4 %collective-permute-start.11 = (f32[2,2,16,1,128]{4,3,2,0,1:T(1,128)S(1)}, f32[2,2,16,1,128]{4,3,2,0,1:T(1,128)S(1)}, u32[]{:S(2)}, u32[]{:S(2)}) collective-permute-start(f32[2,2,16,1,128]{4,3,2,0,1:T(1,128)S(1)} %slice.680), channel_id=1, source_target_pairs={{0,1},{1,2},{2,3},{3,4},{4,5},{5,6},{6,7},{7,8},{8,9},{9,10},{10,1... | collective-permute-start | bytes 98312 | tf_op jit(solution)/shard_map/ppermute | solution.py:14
  112.4 3.4 %collective-permute-start.14 = (f32[2,2,1,8,128]{4,3,0,2,1:T(8,128)S(1)}, f32[2,2,1,8,128]{4,3,0,2,1:T(8,128)S(1)}, u32[]{:S(2)}, u32[]{:S(2)}) collective-permute-start(f32[2,2,1,8,128]{4,3,0,2,1:T(8,128)S(1)} %copy.349), channel_id=1, source_target_pairs={{0,16},{16,32},{32,48},{48,64},{64,80},{80,96},{96,112},{1,17},{17... | collective-permute-start | bytes 49160 | tf_op jit(solution)/shard_map/ppermute | solution.py:14
  115.8 4.3 %collective-permute-start.15 = (f32[2,2,16,1,128]{4,2,0,3,1:T(8,128)S(1)}, f32[2,2,16,1,128]{4,2,0,3,1:T(8,128)S(1)}, u32[]{:S(2)}, u32[]{:S(2)}) collective-permute-start(f32[2,2,16,1,128]{4,2,0,3,1:T(8,128)S(1)} %copy.351), channel_id=1, source_target_pairs={{0,1},{1,2},{2,3},{3,4},{4,5},{5,6},{6,7},{7,8},{8,9},{9,10},{10,1... | collective-permute-start | bytes 98312 | tf_op jit(solution)/shard_map/ppermute | solution.py:14
  120.2 1.2 collective-permute-done.15
  121.7 2.5 %multiply_add_fusion = (f32[2,3,16,8,128]{4,3,2,0,1:T(8,128)}, f32[16,8,128]{2,1,0:T(8,128)}, f32[2,3,16,8,128]{4,3,2,0,1:T(8,128)S(1)}, f32[2,3,16,8,128]{4,3,2,0,1:T(8,128)S(1)}) fusion(f32[2,3,16,8,128]{4,3,2,0,1:T(8,128)S(1)} %get-tuple-element.18, f32[16,8,128]{2,1,0:T(8,128)S(1)} %get-tuple-element.80, f32[16,8,128]{2,1,0:T(8,128)S(1)} %get-tuple-element.78, ...), kind=kLoop, calls=%fused_computation.24 | loop fusion | flops 1654784 | bytes 3211264 | tf_op jit(solution)/shard_map/add | solution.py:124
  124.2 12.7 %copy.333 = f32[2,3,16,8,128]{1,0,4,3,2:T(2,128)} copy(f32[2,3,16,8,128]{4,3,2,0,1:T(8,128)} %get-tuple-element.21) | data formatting | bytes 786432 | tf_op jit(solution)/shard_map/add | solution.py:124
  137.0 6.5 %gather_fusion.2 = f32[16,2,3]{2,1,0:T(2,128)S(1)} fusion(f32[2,3,16384]{1,0,2:T(2,128)} %bitcast.336, s32[1024]{0:T(1024)} %copy-done.18), kind=kCustom, calls=%fused_computation.2.clone | custom fusion | bytes 832 | tf_op jit(solution)/shard_map/jit(_take)/gather | solution.py:125
  144.7 13.0 %all-to-all-start.2 = ((f32[2,16,2,3]{3,2,0,1:T(2,128)}), f32[2,16,2,3]{3,2,0,1:T(2,128)S(1)}, u32[]{:S(2)}, u32[]{:S(2)}) async-start(f32[2,16,2,3]{3,2,0,1:T(2,128)} %copy.335), calls=%async_computation.2 | async-start | bytes 65536 | tf_op jit(solution)/shard_map/all_to_all | solution.py:128
  158.4 5.8 %all-to-all-done.2 = f32[2,16,2,3]{3,2,0,1:T(2,128)S(1)} async-done(((f32[2,16,2,3]{3,2,0,1:T(2,128)}), f32[2,16,2,3]{3,2,0,1:T(2,128)S(1)}, u32[]{:S(2)}, u32[]{:S(2)}) %all-to-all-start.2) | async-done | bytes 800 | tf_op jit(solution)/shard_map/all_to_all | solution.py:128
  164.2 4.5 %all-to-all-start.1 = ((f32[2,16,2,3]{3,2,0,1:T(2,128)}), f32[2,16,2,3]{3,2,0,1:T(2,128)S(1)}, u32[]{:S(2)}, u32[]{:S(2)}) async-start(f32[2,16,2,3]{3,2,0,1:T(2,128)} %copy.332), calls=%async_computation.1 | async-start | bytes 65536 | tf_op jit(solution)/shard_map/all_to_all | solution.py:128
  170.1 5.1 %all-to-all-done.1 = f32[2,16,2,3]{3,2,0,1:T(2,128)S(1)} async-done(((f32[2,16,2,3]{3,2,0,1:T(2,128)}), f32[2,16,2,3]{3,2,0,1:T(2,128)S(1)}, u32[]{:S(2)}, u32[]{:S(2)}) %all-to-all-start.1) | async-done | bytes 800 | tf_op jit(solution)/shard_map/all_to_all | solution.py:128
  175.3 5.1 %all-to-all-start = ((f32[2,16,2,3]{3,2,0,1:T(2,128)}), f32[2,16,2,3]{3,2,0,1:T(2,128)}, u32[]{:S(2)}, u32[]{:S(2)}) async-start(f32[2,16,2,3]{3,2,0,1:T(2,128)} %copy.329), calls=%async_computation | async-start | bytes 65536 | tf_op jit(solution)/shard_map/all_to_all | solution.py:128
  181.7 1.9 collective-permute-start.16
  183.8 3.1 %collective-permute-start.17 = (f32[2,2,16,1,128]{4,3,2,0,1:T(1,128)}, f32[2,2,16,1,128]{4,3,2,0,1:T(1,128)}, u32[]{:S(2)}, u32[]{:S(2)}) collective-permute-start(f32[2,2,16,1,128]{4,3,2,0,1:T(1,128)} %slice.713), channel_id=1, source_target_pairs={{1,0},{2,1},{3,2},{4,3},{5,4},{6,5},{7,6},{8,7},{9,8},{10,9},{11,1... | collective-permute-start | bytes 98312 | tf_op jit(solution)/shard_map/ppermute | solution.py:14
  188.6 1.4 copy.336
  190.0 1.3 maximum_bitcast_fusion
  194.1 4.6 %collective-permute-start.18 = (f32[2,2,1,8,128]{4,3,0,2,1:T(8,128)S(1)}, f32[2,2,1,8,128]{4,3,0,2,1:T(8,128)S(1)}, u32[]{:S(2)}, u32[]{:S(2)}) collective-permute-start(f32[2,2,1,8,128]{4,3,0,2,1:T(8,128)S(1)} %copy.355), channel_id=1, source_target_pairs={{0,16},{16,32},{32,48},{48,64},{64,80},{80,96},{96,112},{1,17},{17... | collective-permute-start | bytes 49160 | tf_op jit(solution)/shard_map/ppermute | solution.py:14
  198.7 2.2 collective-permute-start.19
  201.0 3.3 %collective-permute-done.19 = f32[2,2,16,1,128]{4,3,2,1,0:T(1,128)S(1)} collective-permute-done((f32[2,2,16,1,128]{4,3,2,1,0:T(1,128)S(1)}, f32[2,2,16,1,128]{4,3,2,1,0:T(1,128)S(1)}, u32[]{:S(2)}, u32[]{:S(2)}) %collective-permute-start.19) | collective-permute-done | bytes 32800 | tf_op jit(solution)/shard_map/ppermute | solution.py:14
  204.5 1.4 multiply_reduce_fusion
  205.9 19.5 %all-gather = f32[64,8,128]{2,1,0:T(8,128)S(1)} all-gather(f32[16,8,128]{2,1,0:T(8,128)S(1)} %add_add_fusion), channel_id=2, replica_groups=mesh['src'=4,'depth'=8,'lat'=16] {'src'}, dimensions={0}, use_global_device_ids=true | all-gather | bytes 327680 | tf_op jit(solution)/shard_map/all_gather | solution.py:147
  (173 shorter events, 31.0 us)
Async XLA Ops:
  1.7 12.4 %collective-permute-start = (f32[2,2,1,8,128]{4,0,3,2,1:T(2,128)S(1)}, f32[2,2,1,8,128]{4,0,3,2,1:T(2,128)S(1)}, u32[]{:S(2)}, u32[]{:S(2)}) collective-permute-start(f32[2,2,1,8,128]{4,0,3,2,1:T(2,128)S(1)} %bitcast.363), channel_id=1, source_target_pairs={{16,0},{32,16},{48,32},{64,48},{80,64},{96,80},{112,96},{17,1},{33... | collective-permute-start | bytes 49160 | tf_op jit(solution)/shard_map/ppermute | solution.py:14
  3.8 10.3 %collective-permute-start.1 = (f32[2,2,16,1,128]{4,2,0,3,1:T(8,128)S(1)}, f32[2,2,16,1,128]{4,2,0,3,1:T(8,128)S(1)}, u32[]{:S(2)}, u32[]{:S(2)}) collective-permute-start(f32[2,2,16,1,128]{4,2,0,3,1:T(8,128)S(1)} %slice.625), channel_id=1, source_target_pairs={{1,0},{2,1},{3,2},{4,3},{5,4},{6,5},{7,6},{8,7},{9,8},{10,9},{11,1... | collective-permute-start | bytes 98312 | tf_op jit(solution)/shard_map/ppermute | solution.py:14
  13.9 11.8 %copy-start.12 = (f32[2,1,16,8,128]{4,3,2,0,1:T(8,128)}, f32[2,1,16,8,128]{4,3,2,0,1:T(8,128)S(1)}, u32[]{:S(2)}) copy-start(f32[2,1,16,8,128]{4,3,2,0,1:T(8,128)S(1)} %get-tuple-element.123) | copy-start | bytes 393220
  13.9 47.0 %copy-start.1 = (f32[2,3,16,8,128]{4,3,2,1,0:T(8,128)S(1)}, f32[2,3,16,8,128]{4,3,2,1,0:T(8,128)}, u32[]{:S(2)}) copy-start(f32[2,3,16,8,128]{4,3,2,1,0:T(8,128)} %param.14) | copy-start | bytes 1179652
  13.9 35.9 %copy-start.18 = (s32[1024]{0:T(1024)}, s32[1024]{0:T(1024)S(1)}, u32[]{:S(2)}) copy-start(s32[1024]{0:T(1024)S(1)} %pad_clamp_fusion) | copy-start | bytes 12292
  15.4 7.6 %collective-permute-start.2 = (f32[2,2,1,8,128]{4,0,3,2,1:T(2,128)S(1)}, f32[2,2,1,8,128]{4,0,3,2,1:T(2,128)S(1)}, u32[]{:S(2)}, u32[]{:S(2)}) collective-permute-start(f32[2,2,1,8,128]{4,0,3,2,1:T(2,128)S(1)} %bitcast.364), channel_id=1, source_target_pairs={{0,16},{16,32},{32,48},{48,64},{64,80},{80,96},{96,112},{1,17},{17... | collective-permute-start | bytes 49160 | tf_op jit(solution)/shard_map/ppermute | solution.py:14
  19.9 5.6 %collective-permute-start.3 = (f32[2,2,16,1,128]{4,2,0,3,1:T(8,128)S(1)}, f32[2,2,16,1,128]{4,2,0,3,1:T(8,128)S(1)}, u32[]{:S(2)}, u32[]{:S(2)}) collective-permute-start(f32[2,2,16,1,128]{4,2,0,3,1:T(8,128)S(1)} %slice.636), channel_id=1, source_target_pairs={{0,1},{1,2},{2,3},{3,4},{4,5},{5,6},{6,7},{7,8},{8,9},{9,10},{10,1... | collective-permute-start | bytes 98312 | tf_op jit(solution)/shard_map/ppermute | solution.py:14
  27.0 22.7 %collective-permute-start.4 = (f32[2,2,1,8,128]{4,2,0,3,1:T(1,128)S(1)}, f32[2,2,1,8,128]{4,2,0,3,1:T(1,128)S(1)}, u32[]{:S(2)}, u32[]{:S(2)}) collective-permute-start(f32[2,2,1,8,128]{4,2,0,3,1:T(1,128)S(1)} %slice.643), channel_id=1, source_target_pairs={{16,0},{32,16},{48,32},{64,48},{80,64},{96,80},{112,96},{17,1},{33... | collective-permute-start | bytes 49160 | tf_op jit(solution)/shard_map/ppermute | solution.py:14
  40.6 9.2 %collective-permute-start.5 = (f32[2,2,16,1,128]{4,2,0,3,1:T(8,128)S(1)}, f32[2,2,16,1,128]{4,2,0,3,1:T(8,128)S(1)}, u32[]{:S(2)}, u32[]{:S(2)}) collective-permute-start(f32[2,2,16,1,128]{4,2,0,3,1:T(8,128)S(1)} %slice.647), channel_id=1, source_target_pairs={{1,0},{2,1},{3,2},{4,3},{5,4},{6,5},{7,6},{8,7},{9,8},{10,9},{11,1... | collective-permute-start | bytes 98312 | tf_op jit(solution)/shard_map/ppermute | solution.py:14
  49.9 10.9 %copy-start.6 = (f32[2,1,16,8,128]{4,3,2,0,1:T(8,128)}, f32[2,1,16,8,128]{4,3,2,0,1:T(8,128)S(1)}, u32[]{:S(2)}) copy-start(f32[2,1,16,8,128]{4,3,2,0,1:T(8,128)S(1)} %copy.285) | copy-start | bytes 393220
  50.1 10.8 %copy-start.7 = (f32[2,1,16,8,128]{4,3,2,0,1:T(8,128)}, f32[2,1,16,8,128]{4,3,2,0,1:T(8,128)S(1)}, u32[]{:S(2)}) copy-start(f32[2,1,16,8,128]{4,3,2,0,1:T(8,128)S(1)} %fusion.102) | copy-start | bytes 393220
  50.4 8.0 %collective-permute-start.6 = (f32[2,2,1,8,128]{4,3,0,2,1:T(8,128)S(1)}, f32[2,2,1,8,128]{4,3,0,2,1:T(8,128)S(1)}, u32[]{:S(2)}, u32[]{:S(2)}) collective-permute-start(f32[2,2,1,8,128]{4,3,0,2,1:T(8,128)S(1)} %slice_bitcast_fusion.44), channel_id=1, source_target_pairs={{0,16},{16,32},{32,48},{48,64},{64,80},{80,96},{96,112},{1,17},{17... | collective-permute-start | bytes 49160 | tf_op jit(solution)/shard_map/ppermute | solution.py:14
  55.1 5.6 %collective-permute-start.7 = (f32[2,2,16,1,128]{4,3,2,0,1:T(1,128)S(1)}, f32[2,2,16,1,128]{4,3,2,0,1:T(1,128)S(1)}, u32[]{:S(2)}, u32[]{:S(2)}) collective-permute-start(f32[2,2,16,1,128]{4,3,2,0,1:T(1,128)S(1)} %slice.658), channel_id=1, source_target_pairs={{0,1},{1,2},{2,3},{3,4},{4,5},{5,6},{6,7},{7,8},{8,9},{9,10},{10,1... | collective-permute-start | bytes 98312 | tf_op jit(solution)/shard_map/ppermute | solution.py:14
  60.8 60.8 %copy-start.2 = (f32[2,1,16,8,128]{4,3,2,0,1:T(8,128)}, f32[2,1,16,8,128]{4,3,2,0,1:T(8,128)S(1)}, u32[]{:S(2)}) copy-start(f32[2,1,16,8,128]{4,3,2,0,1:T(8,128)S(1)} %get-tuple-element.33) | copy-start | bytes 393220
  60.8 60.8 %copy-start.4 = (f32[2,1,16,8,128]{4,3,2,0,1:T(8,128)}, f32[2,1,16,8,128]{4,3,2,0,1:T(8,128)S(1)}, u32[]{:S(2)}) copy-start(f32[2,1,16,8,128]{4,3,2,0,1:T(8,128)S(1)} %get-tuple-element.34) | copy-start | bytes 393220
  61.7 12.1 %copy-start.10 = (f32[2,16,8,128]{3,2,1,0:T(8,128)}, f32[2,16,8,128]{3,2,1,0:T(8,128)S(1)}, u32[]{:S(2)}) copy-start(f32[2,16,8,128]{3,2,1,0:T(8,128)S(1)} %get-tuple-element.46) | copy-start | bytes 393220
  61.7 14.0 %copy-start.11 = (f32[2,16,8,128]{3,2,1,0:T(8,128)}, f32[2,16,8,128]{3,2,1,0:T(8,128)S(1)}, u32[]{:S(2)}) copy-start(f32[2,16,8,128]{3,2,1,0:T(8,128)S(1)} %get-tuple-element.47) | copy-start | bytes 393220
  62.3 31.9 %collective-permute-start.8 = (f32[2,2,1,8,128]{4,3,0,2,1:T(8,128)}, f32[2,2,1,8,128]{4,3,0,2,1:T(8,128)}, u32[]{:S(2)}, u32[]{:S(2)}) collective-permute-start(f32[2,2,1,8,128]{4,3,0,2,1:T(8,128)} %slice_bitcast_fusion.41), channel_id=1, source_target_pairs={{16,0},{32,16},{48,32},{64,48},{80,64},{96,80},{112,96},{17,1},{33... | collective-permute-start | bytes 49160 | tf_op jit(solution)/shard_map/ppermute | solution.py:14
  64.9 7.3 %copy-start.8 = (f32[2,16,8,128]{3,2,1,0:T(8,128)}, f32[2,16,8,128]{3,2,1,0:T(8,128)S(1)}, u32[]{:S(2)}) copy-start(f32[2,16,8,128]{3,2,1,0:T(8,128)S(1)} %get-tuple-element.71) | copy-start | bytes 393220
  64.9 8.0 %copy-start.9 = (f32[2,16,8,128]{3,2,1,0:T(8,128)}, f32[2,16,8,128]{3,2,1,0:T(8,128)S(1)}, u32[]{:S(2)}) copy-start(f32[2,16,8,128]{3,2,1,0:T(8,128)S(1)} %get-tuple-element.72) | copy-start | bytes 393220
  68.4 27.3 %collective-permute-start.9 = (f32[2,2,16,1,128]{4,3,2,0,1:T(1,128)}, f32[2,2,16,1,128]{4,3,2,0,1:T(1,128)}, u32[]{:S(2)}, u32[]{:S(2)}) collective-permute-start(f32[2,2,16,1,128]{4,3,2,0,1:T(1,128)} %slice.669), channel_id=1, source_target_pairs={{1,0},{2,1},{3,2},{4,3},{5,4},{6,5},{7,6},{8,7},{9,8},{10,9},{11,1... | collective-permute-start | bytes 98312 | tf_op jit(solution)/shard_map/ppermute | solution.py:14
  70.3 24.7 %collective-permute-start.12 = (f32[2,2,1,8,128]{4,3,0,2,1:T(8,128)}, f32[2,2,1,8,128]{4,3,0,2,1:T(8,128)}, u32[]{:S(2)}, u32[]{:S(2)}) collective-permute-start(f32[2,2,1,8,128]{4,3,0,2,1:T(8,128)} %slice_bitcast_fusion.35), channel_id=1, source_target_pairs={{16,0},{32,16},{48,32},{64,48},{80,64},{96,80},{112,96},{17,1},{33... | collective-permute-start | bytes 49160 | tf_op jit(solution)/shard_map/ppermute | solution.py:14
  73.7 30.9 %collective-permute-start.13 = (f32[2,2,16,1,128]{4,3,2,0,1:T(1,128)}, f32[2,2,16,1,128]{4,3,2,0,1:T(1,128)}, u32[]{:S(2)}, u32[]{:S(2)}) collective-permute-start(f32[2,2,16,1,128]{4,3,2,0,1:T(1,128)} %slice.691), channel_id=1, source_target_pairs={{1,0},{2,1},{3,2},{4,3},{5,4},{6,5},{7,6},{8,7},{9,8},{10,9},{11,1... | collective-permute-start | bytes 98312 | tf_op jit(solution)/shard_map/ppermute | solution.py:14
  100.1 20.0 %collective-permute-start.10 = (f32[2,2,1,8,128]{4,3,0,2,1:T(8,128)S(1)}, f32[2,2,1,8,128]{4,3,0,2,1:T(8,128)S(1)}, u32[]{:S(2)}, u32[]{:S(2)}) collective-permute-start(f32[2,2,1,8,128]{4,3,0,2,1:T(8,128)S(1)} %slice_bitcast_fusion.38), channel_id=1, source_target_pairs={{0,16},{16,32},{32,48},{48,64},{64,80},{80,96},{96,112},{1,17},{17... | collective-permute-start | bytes 49160 | tf_op jit(solution)/shard_map/ppermute | solution.py:14
  106.5 98.0 %copy-start = (f32[2,3,16,8,128]{4,3,2,1,0:T(8,128)S(1)}, f32[2,3,16,8,128]{4,3,2,1,0:T(8,128)}, u32[]{:S(2)}) copy-start(f32[2,3,16,8,128]{4,3,2,1,0:T(8,128)} %param.12) | copy-start | bytes 1179652
  109.0 11.1 %collective-permute-start.11 = (f32[2,2,16,1,128]{4,3,2,0,1:T(1,128)S(1)}, f32[2,2,16,1,128]{4,3,2,0,1:T(1,128)S(1)}, u32[]{:S(2)}, u32[]{:S(2)}) collective-permute-start(f32[2,2,16,1,128]{4,3,2,0,1:T(1,128)S(1)} %slice.680), channel_id=1, source_target_pairs={{0,1},{1,2},{2,3},{3,4},{4,5},{5,6},{6,7},{7,8},{8,9},{9,10},{10,1... | collective-permute-start | bytes 98312 | tf_op jit(solution)/shard_map/ppermute | solution.py:14
  112.4 7.7 %collective-permute-start.14 = (f32[2,2,1,8,128]{4,3,0,2,1:T(8,128)S(1)}, f32[2,2,1,8,128]{4,3,0,2,1:T(8,128)S(1)}, u32[]{:S(2)}, u32[]{:S(2)}) collective-permute-start(f32[2,2,1,8,128]{4,3,0,2,1:T(8,128)S(1)} %copy.349), channel_id=1, source_target_pairs={{0,16},{16,32},{32,48},{48,64},{64,80},{80,96},{96,112},{1,17},{17... | collective-permute-start | bytes 49160 | tf_op jit(solution)/shard_map/ppermute | solution.py:14
  115.8 5.6 %collective-permute-start.15 = (f32[2,2,16,1,128]{4,2,0,3,1:T(8,128)S(1)}, f32[2,2,16,1,128]{4,2,0,3,1:T(8,128)S(1)}, u32[]{:S(2)}, u32[]{:S(2)}) collective-permute-start(f32[2,2,16,1,128]{4,2,0,3,1:T(8,128)S(1)} %copy.351), channel_id=1, source_target_pairs={{0,1},{1,2},{2,3},{3,4},{4,5},{5,6},{6,7},{7,8},{8,9},{9,10},{10,1... | collective-permute-start | bytes 98312 | tf_op jit(solution)/shard_map/ppermute | solution.py:14
  124.2 19.2 %copy-start.16 = (f32[16,2,3]{2,1,0:T(2,128)S(1)}, f32[16,2,3]{2,1,0:T(2,128)}, u32[]{:S(2)}) copy-start(f32[16,2,3]{2,1,0:T(2,128)} %gather_fusion) | copy-start | bytes 1156
  124.2 19.2 %copy-start.17 = (f32[16,2,3]{2,1,0:T(2,128)S(1)}, f32[16,2,3]{2,1,0:T(2,128)}, u32[]{:S(2)}) copy-start(f32[16,2,3]{2,1,0:T(2,128)} %gather_fusion.1) | copy-start | bytes 1156
  124.2 19.2 %copy-start.19 = (pred[16]{0:T(512)(128)(4,1)S(1)}, pred[16]{0:T(512)(128)(4,1)}, u32[]{:S(2)}) copy-start(pred[16]{0:T(512)(128)(4,1)} %compare_and_fusion) | copy-start | bytes 52
  124.2 80.3 %copy-start.3 = (f32[2,1,16,8,128]{4,3,2,0,1:T(8,128)S(1)}, f32[2,1,16,8,128]{4,3,2,0,1:T(8,128)}, u32[]{:S(2)}) copy-start(f32[2,1,16,8,128]{4,3,2,0,1:T(8,128)} %copy-done.2) | copy-start | bytes 393220
  124.2 80.3 %copy-start.5 = (f32[2,1,16,8,128]{4,3,2,0,1:T(8,128)S(1)}, f32[2,1,16,8,128]{4,3,2,0,1:T(8,128)}, u32[]{:S(2)}) copy-start(f32[2,1,16,8,128]{4,3,2,0,1:T(8,128)} %copy-done.4) | copy-start | bytes 393220
  124.2 81.7 %copy-start.13 = (f32[16,8,128]{2,1,0:T(8,128)S(1)}, f32[16,8,128]{2,1,0:T(8,128)}, u32[]{:S(2)}) copy-start(f32[16,8,128]{2,1,0:T(8,128)} %get-tuple-element.22) | copy-start | bytes 196612
  144.7 19.5 %all-to-all-start.2 = ((f32[2,16,2,3]{3,2,0,1:T(2,128)}), f32[2,16,2,3]{3,2,0,1:T(2,128)S(1)}, u32[]{:S(2)}, u32[]{:S(2)}) async-start(f32[2,16,2,3]{3,2,0,1:T(2,128)} %copy.335), calls=%async_computation.2 | async-start | bytes 65536 | tf_op jit(solution)/shard_map/all_to_all | solution.py:128
  164.2 4.5 %copy-start.14 = (f32[2,16,2,3]{3,2,0,1:T(2,128)}, f32[2,16,2,3]{3,2,0,1:T(2,128)S(1)}, u32[]{:S(2)}) copy-start(f32[2,16,2,3]{3,2,0,1:T(2,128)S(1)} %all-to-all-done.2) | copy-start | bytes 2308
  164.2 11.1 %all-to-all-start.1 = ((f32[2,16,2,3]{3,2,0,1:T(2,128)}), f32[2,16,2,3]{3,2,0,1:T(2,128)S(1)}, u32[]{:S(2)}, u32[]{:S(2)}) async-start(f32[2,16,2,3]{3,2,0,1:T(2,128)} %copy.332), calls=%async_computation.1 | async-start | bytes 65536 | tf_op jit(solution)/shard_map/all_to_all | solution.py:128
  175.3 8.3 %copy-start.15 = (f32[2,16,2,3]{3,2,0,1:T(2,128)}, f32[2,16,2,3]{3,2,0,1:T(2,128)S(1)}, u32[]{:S(2)}) copy-start(f32[2,16,2,3]{3,2,0,1:T(2,128)S(1)} %all-to-all-done.1) | copy-start | bytes 2308
  175.3 13.3 %all-to-all-start = ((f32[2,16,2,3]{3,2,0,1:T(2,128)}), f32[2,16,2,3]{3,2,0,1:T(2,128)}, u32[]{:S(2)}, u32[]{:S(2)}) async-start(f32[2,16,2,3]{3,2,0,1:T(2,128)} %copy.329), calls=%async_computation | async-start | bytes 65536 | tf_op jit(solution)/shard_map/all_to_all | solution.py:128
  181.7 9.7 %collective-permute-start.16 = (f32[2,2,1,8,128]{4,3,0,2,1:T(8,128)}, f32[2,2,1,8,128]{4,3,0,2,1:T(8,128)}, u32[]{:S(2)}, u32[]{:S(2)}) collective-permute-start(f32[2,2,1,8,128]{4,3,0,2,1:T(8,128)} %slice_bitcast_fusion.32), channel_id=1, source_target_pairs={{16,0},{32,16},{48,32},{64,48},{80,64},{96,80},{112,96},{17,1},{33... | collective-permute-start | bytes 49160 | tf_op jit(solution)/shard_map/ppermute | solution.py:14
  183.8 8.3 %collective-permute-start.17 = (f32[2,2,16,1,128]{4,3,2,0,1:T(1,128)}, f32[2,2,16,1,128]{4,3,2,0,1:T(1,128)}, u32[]{:S(2)}, u32[]{:S(2)}) collective-permute-start(f32[2,2,16,1,128]{4,3,2,0,1:T(1,128)} %slice.713), channel_id=1, source_target_pairs={{1,0},{2,1},{3,2},{4,3},{5,4},{6,5},{7,6},{8,7},{9,8},{10,9},{11,1... | collective-permute-start | bytes 98312 | tf_op jit(solution)/shard_map/ppermute | solution.py:14
  194.1 6.9 %collective-permute-start.18 = (f32[2,2,1,8,128]{4,3,0,2,1:T(8,128)S(1)}, f32[2,2,1,8,128]{4,3,0,2,1:T(8,128)S(1)}, u32[]{:S(2)}, u32[]{:S(2)}) collective-permute-start(f32[2,2,1,8,128]{4,3,0,2,1:T(8,128)S(1)} %copy.355), channel_id=1, source_target_pairs={{0,16},{16,32},{32,48},{48,64},{64,80},{80,96},{96,112},{1,17},{17... | collective-permute-start | bytes 49160 | tf_op jit(solution)/shard_map/ppermute | solution.py:14
  198.7 5.6 %collective-permute-start.19 = (f32[2,2,16,1,128]{4,3,2,1,0:T(1,128)S(1)}, f32[2,2,16,1,128]{4,3,2,1,0:T(1,128)S(1)}, u32[]{:S(2)}, u32[]{:S(2)}) collective-permute-start(f32[2,2,16,1,128]{4,3,2,1,0:T(1,128)S(1)} %slice.724), channel_id=1, source_target_pairs={{0,1},{1,2},{2,3},{3,4},{4,5},{5,6},{6,7},{7,8},{8,9},{9,10},{10,1... | collective-permute-start | bytes 98312 | tf_op jit(solution)/shard_map/ppermute | solution.py:14
